TPU v7x, 32 devices: a whole 2x2x4 slice. The times are simulated.
32 devices in a mesh: dp: 16 (over z, y, x), seq: 2 (over core).
Axes of the slice: x: 2, y: 2, z: 4, core: 2. Of those that a mesh axis runs over, the one named last changes fastest.
Arguments:
- block_in: bfloat16 [16, 256, 768], P('dp', 'seq'), may hold values from -6 to 6
- doc_ids: int32 [16, 256], P('dp', 'seq'), may hold values from 0 to 1, as said below
- positions: int32 [16, 256], P('dp', 'seq'), may hold values from 0 to 223, as said below
- ln1_gain: bfloat16 [768], P(('dp', 'seq')), may hold values from 0.5 to 1.5
- ln1_bias: bfloat16 [768], P(('dp', 'seq')), may hold values from -3 to 3
- qkv_weight: bfloat16 [768, 2304], P(('dp', 'seq')), as said below
- qkv_bias: bfloat16 [2304], P(('dp', 'seq')), may hold values from -3 to 3
- attn_weight: bfloat16 [768, 768], P(('dp', 'seq')), may hold values from -0.875 to 0.875
- attn_bias: bfloat16 [768], P(('dp', 'seq')), may hold values from -3 to 3
- ln2_gain: bfloat16 [768], P(('dp', 'seq')), may hold values from 0.5 to 1.5
- ln2_bias: bfloat16 [768], P(('dp', 'seq')), may hold values from -3 to 3
- fc_weight: bfloat16 [768, 3072], P(('dp', 'seq')), may hold values from -0.21875 to 0.21875
- fc_bias: bfloat16 [3072], P(('dp', 'seq')), may hold values from -3 to 3
- proj_weight: bfloat16 [3072, 768], P(('dp', 'seq')), may hold values from -0.109375 to 0.109375
- proj_bias: bfloat16 [768], P(('dp', 'seq')), may hold values from -3 to 3
- grad_out: bfloat16 [16, 256, 768], P('dp', 'seq'), may hold values from -6 to 6
Outputs:
- block_out: bfloat16 [16, 256, 768], P('dp', 'seq')
- grad_in: bfloat16 [16, 256, 768], P('dp', 'seq')
- grad_ln1_gain: float32 [768], P(('dp', 'seq'))
- grad_ln1_bias: float32 [768], P(('dp', 'seq'))
- grad_qkv_weight: float32 [768, 2304], P(('dp', 'seq'))
- grad_qkv_bias: float32 [2304], P(('dp', 'seq'))
- grad_attn_weight: float32 [768, 768], P(('dp', 'seq'))
- grad_attn_bias: float32 [768], P(('dp', 'seq'))
- grad_ln2_gain: float32 [768], P(('dp', 'seq'))
- grad_ln2_bias: float32 [768], P(('dp', 'seq'))
- grad_fc_weight: float32 [768, 3072], P(('dp', 'seq'))
- grad_fc_bias: float32 [3072], P(('dp', 'seq'))
- grad_proj_weight: float32 [3072, 768], P(('dp', 'seq'))
- grad_proj_bias: float32 [768], P(('dp', 'seq'))
Inputs may be any that keep to these rules, and one draw needn't show every extreme that they name: `doc_ids`: each row holds two documents: id 0 on its first tokens and id 1 on the rest; the first has 32 to 224 tokens. `positions`: each token's index within its document. `qkv_weight`: columns are the query, key and value projections in that order, each with its heads side by side.
All inputs are finite; a program needn't handle non-finite values.
Results may differ from a plain program's by a relative error of at most 0.009.
Values may be sent and summed in bfloat16 or wider, within the bound.
No kernel may reach another device: no remote copies, remote signals or barrier semaphores. Data moves between devices by JAX's collectives and lax.ppermute only.
A program may use at most 192 MiB of HBM per device.

v0:
```python
import math
import jax
import jax.numpy as jnp
from jax import lax
from jax.sharding import PartitionSpec as P

HEADS = 12
HEAD = 64
ROT = 16
EPSILON = 1e-05
ROOT_HALF = 1.0 / math.sqrt(2.0)
ROOT_TWO_PI = 1.0 / math.sqrt(2.0 * math.pi)


def from_behind(shard, axis, by):
    devices = lax.axis_size(axis)
    pairs = [(i, i + by) for i in range(devices) if 0 <= i + by < devices]
    return lax.ppermute(shard, axis, pairs)


def layer_norm(values):
    centred = values - jnp.mean(values, -1, keepdims=True)
    inverse = lax.rsqrt(jnp.mean(centred * centred, -1, keepdims=True) + EPSILON)
    return (centred * inverse, inverse)


def norm_back(upstream, normed, inverse, gain_vec):
    scaled = upstream * gain_vec.astype(jnp.float32)
    return inverse * (
        scaled
        - jnp.mean(scaled, -1, keepdims=True)
        - normed * jnp.mean(scaled * normed, -1, keepdims=True)
    )


def gelu_slope(pre_act):
    return (
        0.5 * (1.0 + lax.erf(pre_act * ROOT_HALF))
        + pre_act * jnp.exp(-0.5 * pre_act * pre_act) * ROOT_TWO_PI
    )


def tables(token_pos):
    half_rot = ROT // 2
    frequency = 10000.0 ** (-(jnp.arange(half_rot).astype(jnp.float32) * 2.0 / ROT))
    angles = token_pos.astype(jnp.float32)[:, None] * frequency[None, :]
    return (jnp.cos(angles)[:, None, :], jnp.sin(angles)[:, None, :])


def rotate(heads, cos_table, sine_table):
    half_rot = ROT // 2
    first = heads[..., :half_rot]
    second = heads[..., half_rot:ROT]
    return jnp.concatenate(
        [
            first * cos_table - second * sine_table,
            second * cos_table + first * sine_table,
            heads[..., ROT:],
        ],
        -1,
    )


def unrotate(heads, cos_table, sine_table):
    half_rot = ROT // 2
    first = heads[..., :half_rot]
    second = heads[..., half_rot:ROT]
    return jnp.concatenate(
        [
            first * cos_table + second * sine_table,
            second * cos_table - first * sine_table,
            heads[..., ROT:],
        ],
        -1,
    )


def local(
    block_in,
    doc_ids,
    positions,
    ln1_gain,
    ln1_bias,
    qkv_weight,
    qkv_bias,
    attn_weight,
    attn_bias,
    ln2_gain,
    ln2_bias,
    fc_weight,
    fc_bias,
    proj_weight,
    proj_bias,
    grad_out,
):
    gathered = (
        lax.all_gather(ln1_gain, ("dp", "seq"), axis=0, tiled=True),
        lax.all_gather(ln1_bias, ("dp", "seq"), axis=0, tiled=True),
        lax.all_gather(qkv_weight, ("dp", "seq"), axis=0, tiled=True),
        lax.all_gather(qkv_bias, ("dp", "seq"), axis=0, tiled=True),
        lax.all_gather(attn_weight, ("dp", "seq"), axis=0, tiled=True),
        lax.all_gather(attn_bias, ("dp", "seq"), axis=0, tiled=True),
        lax.all_gather(ln2_gain, ("dp", "seq"), axis=0, tiled=True),
        lax.all_gather(ln2_bias, ("dp", "seq"), axis=0, tiled=True),
        lax.all_gather(fc_weight, ("dp", "seq"), axis=0, tiled=True),
        lax.all_gather(fc_bias, ("dp", "seq"), axis=0, tiled=True),
        lax.all_gather(proj_weight, ("dp", "seq"), axis=0, tiled=True),
        lax.all_gather(proj_bias, ("dp", "seq"), axis=0, tiled=True),
    )
    (
        norm1_gain,
        norm1_bias,
        qkv_mat,
        qkv_vec,
        out_mat,
        out_vec,
        norm2_gain,
        norm2_bias,
        fc_mat,
        fc_vec,
        proj_mat,
        proj_vec,
    ) = gathered
    row_count, local_len, model_width = block_in.shape
    tokens = row_count * local_len
    offset = lax.axis_index("seq") * local_len
    score_scale = HEAD ** (-0.5)
    float_type = jnp.float32
    inputs = block_in.reshape(tokens, model_width).astype(float_type)
    normed, inverse = layer_norm(inputs)
    acts1 = (normed * norm1_gain.astype(float_type) + norm1_bias.astype(float_type)).astype(
        jnp.bfloat16
    )
    acts2 = (normed * norm2_gain.astype(float_type) + norm2_bias.astype(float_type)).astype(
        jnp.bfloat16
    )
    projected = jnp.dot(acts1, qkv_mat, preferred_element_type=float_type) + qkv_vec.astype(
        float_type
    )
    cos_table, sine_table = tables(positions.reshape(tokens))
    queries = rotate(
        projected[:, :model_width].reshape(tokens, HEADS, HEAD), cos_table, sine_table
    ).astype(jnp.bfloat16)
    keys_own = (
        rotate(
            projected[:, model_width : 2 * model_width].reshape(tokens, HEADS, HEAD),
            cos_table,
            sine_table,
        )
        .astype(jnp.bfloat16)
        .reshape(row_count, local_len, model_width)
    )
    values_own = (
        projected[:, 2 * model_width :]
        .astype(jnp.bfloat16)
        .reshape(row_count, local_len, model_width)
    )
    docs_own = doc_ids.astype(jnp.bfloat16)
    keys_prev, values_prev, docs_prev = from_behind((keys_own, values_own, docs_own), "seq", 1)
    keys_all = jnp.concatenate([keys_prev, keys_own], 1).reshape(
        row_count, 2 * local_len, HEADS, HEAD
    )
    values_all = jnp.concatenate([values_prev, values_own], 1).reshape(
        row_count, 2 * local_len, HEADS, HEAD
    )
    docs_all = jnp.concatenate([docs_prev, docs_own], 1)
    query_heads = queries.reshape(row_count, local_len, HEADS, HEAD)
    query_index = offset + jnp.arange(local_len)
    key_index = offset - local_len + jnp.arange(2 * local_len)
    allowed = (key_index[None, :] <= query_index[:, None]) & (key_index[None, :] >= 0)
    allowed = (allowed[None] & (docs_all[:, None, :] == docs_own[:, :, None]))[:, None]

    def scores_of():
        raw_scores = (
            jnp.einsum("rqhd,rkhd->rhqk", query_heads, keys_all, preferred_element_type=float_type)
            * score_scale
        )
        return jnp.where(allowed, raw_scores, -jnp.inf)

    scores = scores_of()
    row_max = jnp.max(scores, -1, keepdims=True)
    logsum = row_max + jnp.log(jnp.sum(jnp.exp(scores - row_max), -1, keepdims=True))
    probs = jnp.exp(scores - logsum).astype(jnp.bfloat16)
    context = (
        jnp.einsum("rhqk,rkhd->rqhd", probs, values_all, preferred_element_type=float_type)
        .astype(jnp.bfloat16)
        .reshape(tokens, model_width)
    )
    pre_act = jnp.dot(acts2, fc_mat, preferred_element_type=float_type) + fc_vec.astype(float_type)
    hidden = jax.nn.gelu(pre_act, approximate=False).astype(jnp.bfloat16)
    attn_out = jnp.dot(context, out_mat, preferred_element_type=float_type) + out_vec.astype(
        float_type
    )
    mlp_out = jnp.dot(hidden, proj_mat, preferred_element_type=float_type) + proj_vec.astype(
        float_type
    )
    block_out = (
        (inputs + attn_out + mlp_out)
        .astype(jnp.bfloat16)
        .reshape(row_count, local_len, model_width)
    )
    (
        norm1_gain,
        norm1_bias,
        qkv_mat,
        qkv_vec,
        out_mat,
        out_vec,
        norm2_gain,
        norm2_bias,
        fc_mat,
        fc_vec,
        proj_mat,
        proj_vec,
    ) = gathered
    upstream_b = grad_out.reshape(tokens, model_width)
    upstream = upstream_b.astype(float_type)
    grad_proj_bias = jnp.sum(upstream, 0)
    grad_proj_weight = jnp.einsum(
        "nf,nd->fd", hidden, upstream_b, preferred_element_type=float_type
    )
    d_pre = jnp.einsum(
        "nd,fd->nf", upstream_b, proj_mat, preferred_element_type=float_type
    ) * gelu_slope(pre_act)
    grad_fc_bias = jnp.sum(d_pre, 0)
    d_pre_b = d_pre.astype(jnp.bfloat16)
    grad_fc_weight = jnp.einsum("nd,nf->df", acts2, d_pre_b, preferred_element_type=float_type)
    d_acts2 = jnp.einsum("nf,df->nd", d_pre_b, fc_mat, preferred_element_type=float_type)
    grad_ln2_gain = jnp.sum(d_acts2 * normed, 0)
    grad_ln2_bias = jnp.sum(d_acts2, 0)
    grad_attn_bias = jnp.sum(upstream, 0)
    grad_attn_weight = jnp.einsum(
        "nc,nd->cd", context, upstream_b, preferred_element_type=float_type
    )
    d_context = jnp.einsum(
        "nd,cd->nc", upstream_b, out_mat, preferred_element_type=float_type
    ).astype(jnp.bfloat16)
    d_ctx_heads = d_context.reshape(row_count, local_len, HEADS, HEAD)
    row_dot = jnp.sum(
        d_ctx_heads.astype(float_type)
        * context.reshape(row_count, local_len, HEADS, HEAD).astype(float_type),
        -1,
    )
    scores = scores_of()
    weights_full = jnp.exp(scores - logsum)
    d_weights = jnp.einsum(
        "rqhd,rkhd->rhqk", d_ctx_heads, values_all, preferred_element_type=float_type
    )
    d_scores = (
        weights_full * (d_weights - jnp.transpose(row_dot, (0, 2, 1))[..., None]) * score_scale
    ).astype(jnp.bfloat16)
    d_query = jnp.einsum("rhqk,rkhd->rqhd", d_scores, keys_all, preferred_element_type=float_type)
    d_keys = jnp.einsum(
        "rhqk,rqhd->rkhd", d_scores, query_heads, preferred_element_type=float_type
    ).reshape(row_count, 2 * local_len, model_width)
    d_values = jnp.einsum(
        "rhqk,rqhd->rkhd", probs, d_ctx_heads, preferred_element_type=float_type
    ).reshape(row_count, 2 * local_len, model_width)
    back_keys, back_values = (
        from_behind(d_keys[:, :local_len].astype(jnp.bfloat16), "seq", -1).astype(jnp.float32),
        from_behind(d_values[:, :local_len].astype(jnp.bfloat16), "seq", -1).astype(jnp.float32),
    )
    d_keys_own = (d_keys[:, local_len:] + back_keys).reshape(tokens, HEADS, HEAD)
    d_values_own = (d_values[:, local_len:] + back_values).reshape(tokens, model_width)
    d_projected = jnp.concatenate(
        [
            unrotate(d_query.reshape(tokens, HEADS, HEAD), cos_table, sine_table).reshape(
                tokens, model_width
            ),
            unrotate(d_keys_own, cos_table, sine_table).reshape(tokens, model_width),
            d_values_own,
        ],
        1,
    )
    grad_qkv_bias = jnp.sum(d_projected, 0)
    d_proj_b = d_projected.astype(jnp.bfloat16)
    grad_qkv_weight = jnp.einsum("nd,ne->de", acts1, d_proj_b, preferred_element_type=float_type)
    d_acts1 = jnp.einsum("ne,de->nd", d_proj_b, qkv_mat, preferred_element_type=float_type)
    grad_ln1_gain = jnp.sum(d_acts1 * normed, 0)
    grad_ln1_bias = jnp.sum(d_acts1, 0)
    grad_in = (
        (
            upstream
            + norm_back(d_acts1, normed, inverse, norm1_gain)
            + norm_back(d_acts2, normed, inverse, norm2_gain)
        )
        .astype(jnp.bfloat16)
        .reshape(row_count, local_len, model_width)
    )
    summed = (
        lax.psum_scatter(grad_ln1_gain, ("dp", "seq"), scatter_dimension=0, tiled=True),
        lax.psum_scatter(grad_ln1_bias, ("dp", "seq"), scatter_dimension=0, tiled=True),
        lax.psum_scatter(grad_qkv_weight, ("dp", "seq"), scatter_dimension=0, tiled=True),
        lax.psum_scatter(grad_qkv_bias, ("dp", "seq"), scatter_dimension=0, tiled=True),
        lax.psum_scatter(grad_attn_weight, ("dp", "seq"), scatter_dimension=0, tiled=True),
        lax.psum_scatter(grad_attn_bias, ("dp", "seq"), scatter_dimension=0, tiled=True),
        lax.psum_scatter(grad_ln2_gain, ("dp", "seq"), scatter_dimension=0, tiled=True),
        lax.psum_scatter(grad_ln2_bias, ("dp", "seq"), scatter_dimension=0, tiled=True),
        lax.psum_scatter(grad_fc_weight, ("dp", "seq"), scatter_dimension=0, tiled=True),
        lax.psum_scatter(grad_fc_bias, ("dp", "seq"), scatter_dimension=0, tiled=True),
        lax.psum_scatter(grad_proj_weight, ("dp", "seq"), scatter_dimension=0, tiled=True),
        lax.psum_scatter(grad_proj_bias, ("dp", "seq"), scatter_dimension=0, tiled=True),
    )
    return (
        block_out,
        grad_in,
        summed[0],
        summed[1],
        summed[2],
        summed[3],
        summed[4],
        summed[5],
        summed[6],
        summed[7],
        summed[8],
        summed[9],
        summed[10],
        summed[11],
    )


def solution(mesh):
    placed = (
        P("dp", "seq", None),
        P("dp", "seq"),
        P("dp", "seq"),
        P(("dp", "seq")),
        P(("dp", "seq")),
        P(("dp", "seq"), None),
        P(("dp", "seq")),
        P(("dp", "seq"), None),
        P(("dp", "seq")),
        P(("dp", "seq")),
        P(("dp", "seq")),
        P(("dp", "seq"), None),
        P(("dp", "seq")),
        P(("dp", "seq"), None),
        P(("dp", "seq")),
        P("dp", "seq", None),
    )
    return jax.shard_map(
        local,
        mesh=mesh,
        in_specs=placed,
        out_specs=(
            P("dp", "seq", None),
            P("dp", "seq", None),
            P(("dp", "seq")),
            P(("dp", "seq")),
            P(("dp", "seq"), None),
            P(("dp", "seq")),
            P(("dp", "seq"), None),
            P(("dp", "seq")),
            P(("dp", "seq")),
            P(("dp", "seq")),
            P(("dp", "seq"), None),
            P(("dp", "seq")),
            P(("dp", "seq"), None),
            P(("dp", "seq")),
        ),
        check_vma=False,
    )
```

profile of v0, /device:TPU:0, one launch (start us, length us, event | category | flops | bytes accessed | tf_op | source)
XLA Modules:
  0.0 778.8 jit_solution(5045780520184419339)
XLA Ops:
  10.7 2.4 collective-permute-start.1
  19.8 42.1 %all-reduce.16 = (bf16[3072]{0:T(1024)(128)(2,1)}, bf16[768]{0:T(1024)(128)(2,1)}, bf16[768]{0:T(1024)(128)(2,1)}, bf16[768]{0:T(1024)(128)(2,1)}, bf16[2304]{0:...) all-reduce(bf16[3072]{0:T(1024)(128)(2,1)S(1)} %dynamic-update-slic, ...), channel_id=1, replica_groups=mesh['dp'=16,'seq'=2] {'dp','seq'}, use_global_device_ids=true, to_apply=%add.6 | all-reduce | flops 9984 | bytes 39936
  65.7 2.0 all-gather.7.cloned.1.call-done
  67.8 1.9 convolution_convert_fusion
  69.8 59.9 %all-gather.5.cloned.1.call-done = bf16[768,2304]{1,0:T(8,128)(2,1)} async-done(((bf16[24,2304]{1,0:T(8,128)(2,1)}), bf16[768,2304]{1,0:T(8,128)(2,1)}) %all-gather.5.cloned.1.call-update) | async-done | bytes 3538960 | tf_op jit(solution)/shard_map/all_gather | solution.py:99
  129.7 2.7 convolution_add_fusion
  132.9 2.2 collective-permute-start
  140.7 1.8 fusion.57
  147.9 1.6 collective-permute-done.3
  150.2 4.1 fusion.68
  155.0 40.0 %all-gather.9.cloned.1.call-done = bf16[768,3072]{1,0:T(8,128)(2,1)} async-done(((bf16[24,3072]{1,0:T(8,128)(2,1)}), bf16[768,3072]{1,0:T(8,128)(2,1)}) %all-gather.9.cloned.1.call-update) | async-done | bytes 4718608 | tf_op jit(solution)/shard_map/all_gather | solution.py:105
  195.1 7.6 fusion.2
  202.7 57.1 %all-gather.11.cloned.1.call-done = bf16[3072,768]{1,0:T(8,128)(2,1)} async-done(((bf16[96,768]{1,0:T(8,128)(2,1)}), bf16[3072,768]{1,0:T(8,128)(2,1)}) %all-gather.11.cloned.1.call-update) | async-done | bytes 4718608 | tf_op jit(solution)/shard_map/all_gather | solution.py:107
  259.8 4.6 fusion.78
  264.4 5.1 fusion.48
  269.6 5.1 fusion.55
  275.7 4.2 fusion.50
  279.9 1.5 fusion.44
  282.5 40.1 %all-reduce.15 = (f32[768]{0:T(1024)S(1)}, f32[768]{0:T(1024)S(1)}, f32[2304]{0:T(1024)S(1)}, f32[768]{0:T(1024)S(1)}, f32[768]{0:T(1024)S(1)}, /*index=5*/f32[768]{0:T(1024)S(1)}, f32[3072]{0:T(1024)S(1)}) all-reduce(f32[768]{0:T(1024)S(1)} %get-tuple-element.16, ...), channel_id=2, replica_groups=mesh['dp'=16,'seq'=2] {'dp','seq'}, use_global_device_ids=true, to_apply=%region_10.11.clone | all-reduce | flops 9216 | bytes 73728
  326.2 3.2 convolution_add_fusion.3
  330.6 32.9 %reduce-scatter.7.cloned.1.call-done = f32[24,768]{1,0:T(8,128)} async-done(((f32[768,768]{1,0:T(8,128)}), f32[24,768]{1,0:T(8,128)}) %reduce-scatter.7.cloned.1.call-update) | async-done | bytes 73744 | tf_op jit(solution)/shard_map/reduce_scatter | solution.py:295
  363.5 124.8 %reduce-scatter.5.cloned.1.call-done = f32[24,2304]{1,0:T(8,128)} async-done(((f32[768,2304]{1,0:T(8,128)}), f32[24,2304]{1,0:T(8,128)}) %reduce-scatter.5.cloned.1.call-update) | async-done | bytes 221200 | tf_op jit(solution)/shard_map/reduce_scatter | solution.py:293
  488.3 141.6 %reduce-scatter.9.cloned.1.call-done = f32[24,3072]{1,0:T(8,128)} async-done(((f32[768,3072]{1,0:T(8,128)}), f32[24,3072]{1,0:T(8,128)}) %reduce-scatter.9.cloned.1.call-update) | async-done | bytes 294928 | tf_op jit(solution)/shard_map/reduce_scatter | solution.py:299
  629.9 141.6 %reduce-scatter.11.cloned.1.call-done = f32[96,768]{1,0:T(8,128)} async-done(((f32[3072,768]{1,0:T(8,128)}), f32[96,768]{1,0:T(8,128)}) %reduce-scatter.11.cloned.1.call-update) | async-done | bytes 294928 | tf_op jit(solution)/shard_map/reduce_scatter | solution.py:301
  (159 shorter events, 33.7 us)
Async XLA Ops:
  7.2 60.6 %all-gather.7.cloned.1.call-start = ((), (), s32[]{:S(2)}) async-start(), calls=%async_computation.5 | async-start | bytes 1216512 | tf_op jit(solution)/shard_map/all_gather | solution.py:101
  7.9 121.8 %copy-start = (bf16[1,128,768]{2,1,0:T(8,128)(2,1)S(1)}, bf16[1,128,768]{2,1,0:T(8,128)(2,1)}, u32[]{:S(2)}) copy-start(bf16[1,128,768]{2,1,0:T(8,128)(2,1)} %param.16) | copy-start | bytes 589828
  7.9 121.8 %all-gather.5.cloned.1.call-start = ((), (), s32[]{:S(2)}) async-start(), calls=%async_computation.4 | async-start | bytes 3649536 | tf_op jit(solution)/shard_map/all_gather | solution.py:99
  8.7 186.4 %all-gather.9.cloned.1.call-start = ((), (), s32[]{:S(2)}) async-start(), calls=%async_computation.6 | async-start | bytes 4866048 | tf_op jit(solution)/shard_map/all_gather | solution.py:105
  9.4 250.4 %all-gather.11.cloned.1.call-start = ((), (), s32[]{:S(2)}) async-start(), calls=%async_computation.7 | async-start | bytes 4866048 | tf_op jit(solution)/shard_map/all_gather | solution.py:107
  10.0 353.5 %reduce-scatter.7.cloned.1.call-start = ((), (), s32[]{:S(2)}) async-start(), calls=%async_computation.9 | async-start | bytes 2433024 | tf_op jit(solution)/shard_map/reduce_scatter | solution.py:295
  10.7 54.3 %collective-permute-start.1 = (bf16[1,128]{1,0:T(2,128)(2,1)S(1)}, bf16[1,128]{1,0:T(2,128)(2,1)S(1)}, u32[]{:S(2)}, u32[]{:S(2)}) collective-permute-start(bf16[1,128]{1,0:T(2,128)(2,1)S(1)} %get-tuple-element.60), channel_id=1, source_target_pairs={{0,1},{2,3},{4,5},{6,7},{8,9},{10,11},{12,13},{14,15},{16,17},{18,... | collective-permute-start | bytes 776 | tf_op jit(solution)/shard_map/ppermute | solution.py:18
  63.0 66.7 %copy-start.15 = (f32[128]{0:T(128)}, f32[128]{0:T(128)S(1)}, u32[]{:S(2)}) copy-start(f32[128]{0:T(128)S(1)} %broadcast_multiply_fusion.4) | copy-start | bytes 1540
  64.8 64.9 %copy-start.17 = (f32[128]{0:T(128)}, f32[128]{0:T(128)S(1)}, u32[]{:S(2)}) copy-start(f32[128]{0:T(128)S(1)} %add_rsqrt_fusion) | copy-start | bytes 1540
  64.9 70.4 %copy-start.10 = (f32[128,8]{0,1:T(8,128)}, f32[128,8]{0,1:T(8,128)S(1)}, u32[]{:S(2)}) copy-start(f32[128,8]{0,1:T(8,128)S(1)} %get-tuple-element.57) | copy-start | bytes 12292
  64.9 70.4 %copy-start.12 = (f32[128,8]{0,1:T(8,128)}, f32[128,8]{0,1:T(8,128)S(1)}, u32[]{:S(2)}) copy-start(f32[128,8]{0,1:T(8,128)S(1)} %get-tuple-element.58) | copy-start | bytes 12292
  132.9 3.8 collective-permute-start
  135.3 3.7 copy-start.6
  135.4 3.7 copy-start.8
  135.4 2.4 collective-permute-start.2
  142.6 345.8 %reduce-scatter.5.cloned.1.call-start = ((), (), s32[]{:S(2)}) async-start(), calls=%async_computation.8 | async-start | bytes 7299072 | tf_op jit(solution)/shard_map/reduce_scatter | solution.py:293
  144.8 4.7 copy-start.11
  144.8 4.7 copy-start.13
  144.8 4.9 collective-permute-start.4
  146.1 3.3 collective-permute-start.3
  154.4 475.5 %reduce-scatter.9.cloned.1.call-start = ((), (), s32[]{:S(2)}) async-start(), calls=%async_computation.10 | async-start | bytes 9732096 | tf_op jit(solution)/shard_map/reduce_scatter | solution.py:299
  269.5 502.0 %reduce-scatter.11.cloned.1.call-start = ((), (), s32[]{:S(2)}) async-start(), calls=%async_computation.11 | async-start | bytes 9732096 | tf_op jit(solution)/shard_map/reduce_scatter | solution.py:301
  275.7 4.2 copy-start.2
  323.3 448.2 %copy-start.26 = (f32[24]{0:T(128)}, f32[24]{0:T(128)S(1)}, u32[]{:S(2)}) copy-start(f32[24]{0:T(128)S(1)} %dynamic-slice.3) | copy-start | bytes 292
  (16 other events, 26.1 us)
Sparse Core Ops, SparseCore 0:
  10.9 56.8 all-gather.6
  70.7 59.0 all-gather.4
  132.6 62.3 all-gather.8
  197.8 61.9 all-gather.10
  265.5 97.9 reduce-scatter.6
  369.6 118.6 reduce-scatter.4
  494.8 135.0 reduce-scatter.8
  636.3 135.1 reduce-scatter.10
where the time goes:
time: 780 us; the launch traced here: 779 us
  waiting for transfers between devices  605 us (78%)
  blocking collectives  82.2 us (11%)
  matrix products  47.1 us (6%)
  between operations  14.8 us (2%)
  local copies, waits for them, and re-layouts  14.1 us (2%)
  starting transfers between devices  8.92 us (1%)
    reduce_scatter x1, waiting for transfers between devices, local(): lax.psum_scatter(grad_proj_weight, ('dp', 'seq'), scatter_dimension=0, ti...  142 us
    reduce_scatter x1, waiting for transfers between devices, local(): lax.psum_scatter(grad_fc_weight, ('dp', 'seq'), scatter_dimension=0, tile...  142 us
    reduce_scatter x1, waiting for transfers between devices, local(): lax.psum_scatter(grad_qkv_weight, ('dp', 'seq'), scatter_dimension=0, til...  125 us
    unnamed x2, blocking collectives  82.2 us
    all_gather x1, waiting for transfers between devices, local(): lax.all_gather(qkv_weight, ('dp', 'seq'), axis=0, tiled=True)  59.9 us
    all_gather x1, waiting for transfers between devices, local(): lax.all_gather(proj_weight, ('dp', 'seq'), axis=0, tiled=True)  57.1 us
    all_gather x1, waiting for transfers between devices, local(): lax.all_gather(fc_weight, ('dp', 'seq'), axis=0, tiled=True)  40 us
    reduce_scatter x1, waiting for transfers between devices, local(): lax.psum_scatter(grad_attn_weight, ('dp', 'seq'), scatter_dimension=0, ti...  32.9 us
  transfers between devices with their start and end apart: 13, of which 10 were waited for; matrix products, arithmetic and copies ran while one was open for 8% of the time, Pallas kernels for 0%

commit v1 on v0

--- a/solution.py
+++ b/solution.py
@@ -10,6 +10,11 @@
 EPSILON = 1e-05
 ROOT_HALF = 1.0 / math.sqrt(2.0)
 ROOT_TWO_PI = 1.0 / math.sqrt(2.0 * math.pi)
+
+
+def gather_by_exchange(x, axis, dim):
+    copies = jnp.concatenate([x] * lax.axis_size(axis), axis=dim)
+    return lax.all_to_all(copies, axis, dim, dim, tiled=True)
 
 
 def from_behind(shard, axis, by):
@@ -104,7 +109,7 @@
         lax.all_gather(ln2_bias, ("dp", "seq"), axis=0, tiled=True),
         lax.all_gather(fc_weight, ("dp", "seq"), axis=0, tiled=True),
         lax.all_gather(fc_bias, ("dp", "seq"), axis=0, tiled=True),
-        lax.all_gather(proj_weight, ("dp", "seq"), axis=0, tiled=True),
+        gather_by_exchange(proj_weight, ("dp", "seq"), 0),
         lax.all_gather(proj_bias, ("dp", "seq"), axis=0, tiled=True),
     )
     (

time: 780 us -> 750 us (0.962)
  waiting for transfers between devices: 605 us -> 544 us
  local copies, waits for them, and re-layouts: 14.1 us -> 43.3 us
    all_gather x1 -> x0, waiting for transfers between devices: 57.1 us -> none  [local(): lax.all_gather(proj_weight, ('dp', 'seq'), axis=0, tiled=True)]
    all_to_all x0 -> x1, waiting for transfers between devices: none -> 46.3 us  [gather_by_exchange(): return lax.all_to_all(copies, axis, dim, dim, tiled=True)]
    reduce_scatter x1, waiting for transfers between devices: 32.9 us -> 0.01 us  [local(): lax.psum_scatter(grad_attn_weight, ('dp', 'seq'), scatter_dimension=0, ti...]
    unnamed x78 -> x97, local copies, waits for them, and re-layouts: 12.9 us -> 37.3 us
    all_gather x1, waiting for transfers between devices: 40 us -> 58 us  [local(): lax.all_gather(fc_weight, ('dp', 'seq'), axis=0, tiled=True)]
    reduce_scatter x1, waiting for transfers between devices: 125 us -> 108 us  [local(): lax.psum_scatter(grad_qkv_weight, ('dp', 'seq'), scatter_dimension=0, til...]
    all_gather x1, waiting for transfers between devices: 59.9 us -> 44.8 us  [local(): lax.all_gather(qkv_weight, ('dp', 'seq'), axis=0, tiled=True)]
  transfers between devices with their start and end apart: 13 -> 13, of which waited for: 10 -> 8; matrix products, arithmetic and copies ran while one was open for 8% -> 12% of each run, Pallas kernels for 0% -> 0%
where the time goes in v1:
time: 750 us; the launch traced here: 749 us
  waiting for transfers between devices  544 us (73%)
  blocking collectives  80.7 us (11%)
  matrix products  48.1 us (6%)
  local copies, waits for them, and re-layouts  43.3 us (6%)
  between operations  14.7 us (2%)
  starting transfers between devices  13.1 us (2%)
    reduce_scatter x1, waiting for transfers between devices, local(): lax.psum_scatter(grad_proj_weight, ('dp', 'seq'), scatter_dimension=0, ti...  142 us
    reduce_scatter x1, waiting for transfers between devices, local(): lax.psum_scatter(grad_fc_weight, ('dp', 'seq'), scatter_dimension=0, tile...  141 us
    reduce_scatter x1, waiting for transfers between devices, local(): lax.psum_scatter(grad_qkv_weight, ('dp', 'seq'), scatter_dimension=0, til...  108 us
    unnamed x2, blocking collectives  80.7 us
    all_gather x1, waiting for transfers between devices, local(): lax.all_gather(fc_weight, ('dp', 'seq'), axis=0, tiled=True)  58 us
    all_to_all x1, waiting for transfers between devices, gather_by_exchange(): return lax.all_to_all(copies, axis, dim, dim, tiled=True)  46.3 us
    all_gather x1, waiting for transfers between devices, local(): lax.all_gather(qkv_weight, ('dp', 'seq'), axis=0, tiled=True)  44.8 us
    unnamed x97, local copies, waits for them, and re-layouts  37.3 us
  transfers between devices with their start and end apart: 13, of which 8 were waited for; matrix products, arithmetic and copies ran while one was open for 12% of the time, Pallas kernels for 0%

profile of v1, /device:TPU:0, one launch (start us, length us, event | category | flops | bytes accessed | tf_op | source)
XLA Modules:
  0.0 748.7 jit_solution(14867148647906645607)
XLA Ops:
  10.1 2.4 collective-permute-start.1
  19.3 42.2 %all-reduce.16 = (bf16[3072]{0:T(1024)(128)(2,1)}, bf16[768]{0:T(1024)(128)(2,1)}, bf16[768]{0:T(1024)(128)(2,1)}, bf16[768]{0:T(1024)(128)(2,1)}, bf16[2304]{0:...) all-reduce(bf16[3072]{0:T(1024)(128)(2,1)S(1)} %dynamic-update-slic, ...), channel_id=1, replica_groups=mesh['dp'=16,'seq'=2] {'dp','seq'}, use_global_device_ids=true, to_apply=%add.6 | all-reduce | flops 9984 | bytes 39936
  61.4 1.6 constant_dynamic-update-slice_fusion.31
  64.6 1.6 constant_dynamic-update-slice_fusion.29
  66.2 1.6 constant_dynamic-update-slice_fusion.28
  83.1 1.8 convolution_convert_fusion
  85.0 44.8 %all-gather.4.cloned.1.call-done = bf16[768,2304]{1,0:T(8,128)(2,1)} async-done(((bf16[24,2304]{1,0:T(8,128)(2,1)}), bf16[768,2304]{1,0:T(8,128)(2,1)}) %all-gather.4.cloned.1.call-update) | async-done | bytes 3538960 | tf_op jit(solution)/shard_map/all_gather | solution.py:104
  129.8 2.7 convolution_add_fusion
  137.9 2.8 collective-permute-start.2
  146.1 1.8 fusion.58
  152.6 3.6 all-to-all-start
  163.3 4.1 fusion.69
  168.2 58.0 %all-gather.8.cloned.1.call-done = bf16[768,3072]{1,0:T(8,128)(2,1)} async-done(((bf16[24,3072]{1,0:T(8,128)(2,1)}), bf16[768,3072]{1,0:T(8,128)(2,1)}) %all-gather.8.cloned.1.call-update) | async-done | bytes 4718608 | tf_op jit(solution)/shard_map/all_gather | solution.py:110
  226.2 7.6 %fusion.3 = (bf16[128,3072]{1,0:T(8,128)(2,1)S(1)}, f32[128,3072]{1,0:T(8,128)}) fusion(f32[3072]{0:T(1024)S(1)} %convert_element_type.163, bf16[768,3072]{1,0:T(8,128)(2,1)} %all-gather.8.cloned.1.call-done, bf16[1,128,768]{2,1,0:T(8,128)(2,1)S(1)} %copy-done.1, f32[768]{0:T(1024)S(1)} %convert_element_type.161, f32[768]{0:T(1024)S(1)} %convert_element_type.160, ...), kind=kOutput, calls=%fused_computation.8 | convolution fusion | flops 630521856 | bytes 7293952 | tf_op jit(solution)/shard_map/dot_general | solution.py:194
  233.8 46.3 %all-to-all-done = bf16[32,96,768]{2,1,0:T(8,128)(2,1)} async-done(((bf16[32,96,768]{2,1,0:T(8,128)(2,1)}), bf16[32,96,768]{2,1,0:T(8,128)(2,1)}, u32[]{:S(2)}, u32[]{:S(2)}) %all-to-all-start) | async-done | bytes 4718624 | tf_op jit(solution)/shard_map/all_to_all | solution.py:17
  280.1 4.9 fusion.79
  285.0 5.1 fusion.49
  290.2 5.1 fusion.56
  296.4 4.2 fusion.51
  303.1 38.5 %all-reduce.15 = (f32[768]{0:T(1024)S(1)}, f32[768]{0:T(1024)S(1)}, f32[2304]{0:T(1024)S(1)}, f32[768]{0:T(1024)S(1)}, f32[768]{0:T(1024)S(1)}, /*index=5*/f32[768]{0:T(1024)S(1)}, f32[3072]{0:T(1024)S(1)}) all-reduce(f32[768]{0:T(1024)S(1)} %get-tuple-element.16, ...), channel_id=2, replica_groups=mesh['dp'=16,'seq'=2] {'dp','seq'}, use_global_device_ids=true, to_apply=%region_10.11.clone | all-reduce | flops 9216 | bytes 73728
  345.3 3.4 convolution_add_fusion.3
  349.8 108.5 %reduce-scatter.5.cloned.1.call-done = f32[24,2304]{1,0:T(8,128)} async-done(((f32[768,2304]{1,0:T(8,128)}), f32[24,2304]{1,0:T(8,128)}) %reduce-scatter.5.cloned.1.call-update) | async-done | bytes 221200 | tf_op jit(solution)/shard_map/reduce_scatter | solution.py:298
  458.3 141.5 %reduce-scatter.9.cloned.1.call-done = f32[24,3072]{1,0:T(8,128)} async-done(((f32[768,3072]{1,0:T(8,128)}), f32[24,3072]{1,0:T(8,128)}) %reduce-scatter.9.cloned.1.call-update) | async-done | bytes 294928 | tf_op jit(solution)/shard_map/reduce_scatter | solution.py:304
  599.7 141.6 %reduce-scatter.11.cloned.1.call-done = f32[96,768]{1,0:T(8,128)} async-done(((f32[3072,768]{1,0:T(8,128)}), f32[96,768]{1,0:T(8,128)}) %reduce-scatter.11.cloned.1.call-update) | async-done | bytes 294928 | tf_op jit(solution)/shard_map/reduce_scatter | solution.py:306
  (178 shorter events, 58.3 us)
Async XLA Ops:
  7.2 60.6 %copy-start = (bf16[96,768]{1,0:T(8,128)(2,1)S(1)}, bf16[96,768]{1,0:T(8,128)(2,1)}, u32[]{:S(2)}) copy-start(bf16[96,768]{1,0:T(8,128)(2,1)} %param.29) | copy-start | bytes 442372
  7.2 75.9 %all-gather.6.cloned.1.call-start = ((), (), s32[]{:S(2)}) async-start(), calls=%async_computation.6 | async-start | bytes 1216512 | tf_op jit(solution)/shard_map/all_gather | solution.py:106
  7.9 121.9 %all-gather.4.cloned.1.call-start = ((), (), s32[]{:S(2)}) async-start(), calls=%async_computation.5 | async-start | bytes 3649536 | tf_op jit(solution)/shard_map/all_gather | solution.py:104
  8.7 217.5 %all-gather.8.cloned.1.call-start = ((), (), s32[]{:S(2)}) async-start(), calls=%async_computation.7 | async-start | bytes 4866048 | tf_op jit(solution)/shard_map/all_gather | solution.py:110
  9.4 340.3 %reduce-scatter.7.cloned.1.call-start = ((), (), s32[]{:S(2)}) async-start(), calls=%async_computation.9 | async-start | bytes 2433024 | tf_op jit(solution)/shard_map/reduce_scatter | solution.py:300
  10.1 72.2 %collective-permute-start.1 = (bf16[1,128]{1,0:T(2,128)(2,1)S(1)}, bf16[1,128]{1,0:T(2,128)(2,1)S(1)}, u32[]{:S(2)}, u32[]{:S(2)}) collective-permute-start(bf16[1,128]{1,0:T(2,128)(2,1)S(1)} %get-tuple-element.60), channel_id=1, source_target_pairs={{0,1},{2,3},{4,5},{6,7},{8,9},{10,11},{12,13},{14,15},{16,17},{18,... | collective-permute-start | bytes 776 | tf_op jit(solution)/shard_map/ppermute | solution.py:23
  74.4 7.4 copy-start.1
  75.8 6.4 copy-start.19
  75.8 7.3 copy-start.4
  81.9 50.6 %copy-start.10 = (f32[128]{0:T(128)}, f32[128]{0:T(128)S(1)}, u32[]{:S(2)}) copy-start(f32[128]{0:T(128)S(1)} %broadcast_multiply_fusion.4) | copy-start | bytes 1540
  82.1 50.4 %copy-start.12 = (f32[128]{0:T(128)}, f32[128]{0:T(128)S(1)}, u32[]{:S(2)}) copy-start(f32[128]{0:T(128)S(1)} %add_rsqrt_fusion) | copy-start | bytes 1540
  137.9 5.5 collective-permute-start.2
  141.0 2.4 collective-permute-start
  146.0 1.9 copy-start.5
  152.6 127.5 %all-to-all-start = ((bf16[32,96,768]{2,1,0:T(8,128)(2,1)}), bf16[32,96,768]{2,1,0:T(8,128)(2,1)}, u32[]{:S(2)}, u32[]{:S(2)}) async-start(bf16[32,96,768]{2,1,0:T(8,128)(2,1)} %bitcast.18), calls=%async_computation | async-start | bytes 9437184 | tf_op jit(solution)/shard_map/all_to_all | solution.py:17
  156.2 302.1 %reduce-scatter.5.cloned.1.call-start = ((), (), s32[]{:S(2)}) async-start(), calls=%async_computation.8 | async-start | bytes 7299072 | tf_op jit(solution)/shard_map/reduce_scatter | solution.py:298
  156.9 5.9 collective-permute-start.4
  159.2 3.3 collective-permute-start.3
  167.5 432.3 %reduce-scatter.9.cloned.1.call-start = ((), (), s32[]{:S(2)}) async-start(), calls=%async_computation.10 | async-start | bytes 9732096 | tf_op jit(solution)/shard_map/reduce_scatter | solution.py:304
  290.2 451.1 %reduce-scatter.11.cloned.1.call-start = ((), (), s32[]{:S(2)}) async-start(), calls=%async_computation.11 | async-start | bytes 9732096 | tf_op jit(solution)/shard_map/reduce_scatter | solution.py:306
  296.4 4.2 copy-start.3
  342.9 398.4 %copy-start.20 = (f32[24]{0:T(128)}, f32[24]{0:T(128)S(1)}, u32[]{:S(2)}) copy-start(f32[24]{0:T(128)S(1)} %dynamic-slice.3) | copy-start | bytes 292
  345.2 3.4 copy-start.2
  345.3 3.4 copy-start.6
  (10 other events, 8.6 us)
Sparse Core Ops, SparseCore 0:
  10.9 56.8 all-gather.5
  70.7 59.1 all-gather.3
  132.8 93.3 all-gather.7
  231.9 101.4 reduce-scatter.6
  339.5 118.6 reduce-scatter.4
  464.6 135.0 reduce-scatter.8
  606.2 135.0 reduce-scatter.10
